TPU v7x, 512 devices: a whole 4x4x16 slice. The times are simulated.
512 devices in a mesh: nodes: 64 (over x, z), heads: 8 (over y, core).
Axes of the slice: x: 4, y: 4, z: 16, core: 2. Of those that a mesh axis runs over, the one named last changes fastest.
Arguments:
- hidden: bfloat16 [64, 7168], P('nodes'), may hold values from -6 to 6
- norm_gain: float32 [7168], replicated, may hold values from 0.1 to 1.9
- qkv_weight: bfloat16 [7168, 56, 384], P('nodes', 'heads'), may hold values from -0.0625 to 0.0625
- out_weight: bfloat16 [7168, 7168], P('heads', 'nodes'), may hold values from -0.0625 to 0.0625
- prefix_keys: bfloat16 [256, 128, 56, 128], P('nodes', None, 'heads'), may hold values from -1000 to 1000
- prefix_values: bfloat16 [256, 128, 56, 128], P('nodes', None, 'heads'), may hold values from -3 to 3
- leaf_keys: bfloat16 [64, 64, 56, 128], P('nodes', None, 'heads'), may hold values from -1000 to 1000
- leaf_values: bfloat16 [64, 64, 56, 128], P('nodes', None, 'heads'), may hold values from -3 to 3
- piece_node: int32 [256], replicated, may hold values from 0 to 35, as said below
- mid_parent: int32 [32], replicated, may hold values from 0 to 3
- leaf_parent: int32 [64], replicated, may hold values from 0 to 31
- leaf_len: int32 [64], replicated, may hold values from 1 to 64
- sink_len: int32 [64], replicated, may hold values from 0 to 4
- window_len: int32 [64], replicated, may hold values from 2048 to 4096
Outputs:
- layer_out: bfloat16 [64, 7168], P('heads', 'nodes')
Inputs may be any that keep to these rules, and one draw needn't show every extreme that they name: `piece_node`: every root owns some pieces; a middle node may own none.
All inputs are finite; a program needn't handle non-finite values.
Results may differ from a plain program's by a relative error of at most 0.007.
The roundings to bfloat16 on the way count: a program that leaves them out, or rounds other values in their place, can miss the bound.
Values may be sent and summed in bfloat16 or wider, within the bound.
A program may use at most 64 MiB of HBM per device.

v0:
```python
import math
import jax
import jax.numpy as jnp
from jax import lax
from jax.sharding import PartitionSpec as P

SEG = 128
ROOTS = 4
MIDS = 32
epsilon = 1e-05
negative_fill = -1e30


def joined(part, axis, combine):
    gathered = jax.tree.map(lambda a: lax.all_gather(a, axis), part)

    def take(source):
        return jax.tree.map(lambda a: lax.dynamic_index_in_dim(a, source, 0, False), gathered)

    return lax.fori_loop(
        1, lax.axis_size(axis), lambda source, state: combine(state, take(source)), take(0)
    )


def layer_norm(hidden, norm_gain):
    values = hidden.astype(jnp.float32)
    mean_value = jnp.mean(values, axis=1, keepdims=True)
    centered = values - mean_value
    variance = jnp.mean(centered * centered, axis=1, keepdims=True)
    return (centered * lax.rsqrt(variance + epsilon) * norm_gain[None, :]).astype(jnp.bfloat16)


def lookup(lookup_table, chosen):
    positions = jnp.arange(lookup_table.shape[0], dtype=jnp.int32)
    picked = jnp.where(chosen[:, None] == positions[None, :], lookup_table[None, :], 0)
    return jnp.sum(picked, axis=1)


def tree_rows(piece_node, mid_parent, leaf_parent, leaf_len):
    node_ids = jnp.arange(ROOTS + MIDS, dtype=jnp.int32)
    counts = jnp.sum((piece_node[:, None] == node_ids[None, :]).astype(jnp.int32), axis=0)
    root_node = lookup(mid_parent, leaf_parent)
    mid_node = leaf_parent + ROOTS
    root_len = SEG * lookup(counts, root_node)
    mid_len = SEG * lookup(counts, mid_node)
    finish = root_len + mid_len + leaf_len
    return (root_node, mid_node, root_len, finish)


def piece_rank(piece_node, chosen):
    all_pieces = jnp.arange(piece_node.shape[0], dtype=jnp.int32)
    nodes_here = lookup(piece_node, chosen)
    same = (piece_node[None, :] == nodes_here[:, None]) & (all_pieces[None, :] < chosen[:, None])
    return (nodes_here, jnp.sum(same.astype(jnp.int32), axis=1))


def prefix_allowed(
    node_block, rank_block, root_node, mid_node, root_len, finish, sink_len, window_len
):
    offsets = jnp.arange(SEG, dtype=jnp.int32)
    rel_pos = rank_block[:, None] * SEG + offsets[None, :]
    at_root = node_block[None, :] == root_node[:, None]
    at_mid = node_block[None, :] == mid_node[:, None]
    token_pos = rel_pos[None, :, :] + jnp.where(at_mid, root_len[:, None], 0)[:, :, None]
    inside = (token_pos < sink_len[:, None, None]) | (
        token_pos >= (finish - window_len)[:, None, None]
    )
    return ((at_root | at_mid)[:, :, None] & inside)[:, None, :, :]


def leaf_allowed(finish, leaf_len, sink_len, window_len, leaf_max):
    offsets = jnp.arange(leaf_max, dtype=jnp.int32)
    token_pos = (finish - leaf_len)[:, None] + offsets[None, :]
    inside = (token_pos < sink_len[:, None]) | (token_pos >= (finish - window_len)[:, None])
    return (inside & (offsets[None, :] < leaf_len[:, None]))[:, None, :]


def combine(first_part, second_part):
    highest = jnp.maximum(first_part[0], second_part[0])
    factor_one = jnp.exp(first_part[0] - highest)
    factor_two = jnp.exp(second_part[0] - highest)
    totals = first_part[1] * factor_one + second_part[1] * factor_two
    summed = first_part[2] * factor_one[..., None] + second_part[2] * factor_two[..., None]
    return (highest, totals, summed)


def weigh(scores, allowed, axes):
    masked = jnp.where(allowed, scores, negative_fill)
    maxima = jnp.max(masked, axis=axes)
    expanded = maxima
    for axis_pos in axes:
        expanded = jnp.expand_dims(expanded, axis_pos)
    weights = jnp.where(allowed, jnp.exp(masked - expanded), 0.0).astype(jnp.bfloat16)
    return (maxima, weights)


def on_device(
    hidden,
    norm_gain,
    qkv_weight,
    out_weight,
    prefix_keys,
    prefix_values,
    leaf_keys,
    leaf_values,
    piece_node,
    mid_parent,
    leaf_parent,
    leaf_len,
    sink_len,
    window_len,
):
    node_index = lax.axis_index("nodes")
    req_dev = hidden.shape[0]
    heads_dev = qkv_weight.shape[1]
    head_size = qkv_weight.shape[2] // 3
    seg_dev = prefix_keys.shape[0]
    first_row = node_index * req_dev
    score_scale = 1.0 / math.sqrt(head_size)
    normed = layer_norm(hidden, norm_gain)
    columns = lax.all_to_all(normed, "nodes", split_axis=1, concat_axis=0, tiled=True)
    width_here = columns.shape[1]
    flat_weight = qkv_weight.reshape(width_here, heads_dev * 3 * head_size)
    mixed_rows = lax.psum_scatter(
        jnp.dot(columns, flat_weight, preferred_element_type=jnp.float32),
        "nodes",
        scatter_dimension=0,
        tiled=True,
    )
    mixed_rows = mixed_rows.astype(jnp.bfloat16).reshape(req_dev, heads_dev, 3, head_size)
    query_here = mixed_rows[:, :, 0]
    key_new = mixed_rows[:, :, 1]
    value_new = mixed_rows[:, :, 2]
    query_all = lax.all_gather(query_here, "nodes", axis=0, tiled=True)
    root_node, mid_node, root_len, finish = tree_rows(piece_node, mid_parent, leaf_parent, leaf_len)
    chosen = node_index * seg_dev + jnp.arange(seg_dev, dtype=jnp.int32)
    node_block, rank_block = piece_rank(piece_node, chosen)
    scores = (
        jnp.einsum("rhd,pshd->rhps", query_all, prefix_keys, preferred_element_type=jnp.float32)
        * score_scale
    )
    allowed = prefix_allowed(
        node_block, rank_block, root_node, mid_node, root_len, finish, sink_len, window_len
    )
    maxima, weights = weigh(scores, allowed, (2, 3))
    totals = jnp.sum(weights.astype(jnp.float32), axis=(2, 3))
    summed = jnp.einsum(
        "rhps,pshd->rhd", weights, prefix_values, preferred_element_type=jnp.float32
    )
    merged = joined((maxima, totals, summed), "nodes", combine)
    merged = tuple((lax.dynamic_slice_in_dim(member, first_row, req_dev, 0) for member in merged))
    finish_here = lax.dynamic_slice_in_dim(finish, first_row, req_dev, 0)
    leaf_here = lax.dynamic_slice_in_dim(leaf_len, first_row, req_dev, 0)
    sink_here = lax.dynamic_slice_in_dim(sink_len, first_row, req_dev, 0)
    window_here = lax.dynamic_slice_in_dim(window_len, first_row, req_dev, 0)
    leaf_scores = (
        jnp.einsum("rhd,rjhd->rhj", query_here, leaf_keys, preferred_element_type=jnp.float32)
        * score_scale
    )
    leaf_mask = leaf_allowed(finish_here, leaf_here, sink_here, window_here, leaf_keys.shape[1])
    leaf_max, leaf_weights = weigh(leaf_scores, leaf_mask, (2,))
    leaf_part = (
        leaf_max,
        jnp.sum(leaf_weights.astype(jnp.float32), axis=2),
        jnp.einsum("rhj,rjhd->rhd", leaf_weights, leaf_values, preferred_element_type=jnp.float32),
    )
    own_score = (
        jnp.sum(query_here.astype(jnp.float32) * key_new.astype(jnp.float32), axis=2) * score_scale
    )
    own_part = (
        own_score,
        jnp.ones((req_dev, heads_dev), jnp.float32),
        value_new.astype(jnp.float32),
    )
    merged = combine(combine(merged, leaf_part), own_part)
    attended = (
        (merged[2] / merged[1][..., None])
        .astype(jnp.bfloat16)
        .reshape(req_dev, heads_dev * head_size)
    )
    out_rows = jnp.dot(
        lax.all_gather(attended, "nodes", axis=0, tiled=True),
        out_weight,
        preferred_element_type=jnp.float32,
    )
    return lax.psum_scatter(out_rows, "heads", scatter_dimension=0, tiled=True).astype(jnp.bfloat16)


def solution(mesh):
    return jax.shard_map(
        on_device,
        mesh=mesh,
        in_specs=(
            P("nodes", None),
            P(),
            P("nodes", "heads", None),
            P("heads", "nodes"),
            P("nodes", None, "heads", None),
            P("nodes", None, "heads", None),
            P("nodes", None, "heads", None),
            P("nodes", None, "heads", None),
            P(),
            P(),
            P(),
            P(),
            P(),
            P(),
        ),
        out_specs=P("heads", "nodes"),
        check_vma=False,
    )
```

profile of v0, /device:TPU:2, one launch (start us, length us, event | category | flops | bytes accessed | tf_op | source)
XLA Modules:
  0.0 810.2 jit_solution(8103925422148323476)
XLA Ops:
  6.5 1.5 convert_reduce_fusion.3
  8.7 1.4 multiply_reduce_fusion
  12.4 18.6 %all-to-all-start = ((bf16[1,64,112]{2,0,1:T(2,128)(2,1)}), bf16[1,64,112]{2,0,1:T(2,128)(2,1)S(1)}, u32[]{:S(2)}, u32[]{:S(2)}) async-start(bf16[1,64,112]{2,0,1:T(2,128)(2,1)} %all_to_all.15), calls=%async_computation | async-start | bytes 65536 | tf_op jit(solution)/shard_map/all_to_all | solution.py:121
  36.9 1.1 copy.86
  38.0 1.3 dynamic-slice
  39.3 5.2 all-to-all-done
  44.7 257.9 %all-reduce.3 = bf16[64,2688]{1,0:T(8,128)(2,1)S(1)} all-reduce(f32[64,2688]{1,0:T(8,128)S(1)} %fusion.19), channel_id=6, replica_groups=mesh['nodes'=64,'heads'=8] {'nodes'}, use_global_device_ids=true, to_apply=%region_8.9.clone | all-reduce | flops 172032 | bytes 1032192
  303.3 120.7 %all-gather = bf16[64,7,1,128]{3,1,2,0:T(8,128)(2,1)S(1)} all-gather(bf16[1,7,1,128]{3,1,2,0:T(8,128)(2,1)S(1)} %copy.68), channel_id=2, replica_groups=mesh['nodes'=64,'heads'=8] {'nodes'}, dimensions={0}, use_global_device_ids=true | all-gather | bytes 116480 | tf_op jit(solution)/shard_map/all_gather | solution.py:134
  424.5 2.2 convolution_bitcast_fusion
  426.8 1.2 dynamic_slice.68
  428.0 1.3 dynamic_slice.70
  429.3 1.3 dynamic_slice.69
  433.7 1.3 dynamic-slice.2
  435.7 1.3 compare_and_fusion
  437.0 78.9 %all-gather.4 = f32[64,64,7]{1,2,0:T(8,128)S(1)} all-gather(f32[1,64,7]{1,2,0:T(8,128)S(1)} %bitcast.134), channel_id=3, replica_groups=mesh['nodes'=64,'heads'=8] {'nodes'}, dimensions={0}, use_global_device_ids=true | all-gather | bytes 116480 | tf_op jit(solution)/shard_map/all_gather | solution.py:15
  516.2 82.0 %all-gather.5 = f32[64,64,7]{1,2,0:T(8,128)S(1)} all-gather(f32[1,64,7]{1,2,0:T(8,128)S(1)} %bitcast.136), channel_id=4, replica_groups=mesh['nodes'=64,'heads'=8] {'nodes'}, dimensions={0}, use_global_device_ids=true | all-gather | bytes 116480 | tf_op jit(solution)/shard_map/all_gather | solution.py:15
  598.2 1.1 fusion.16
  599.8 1.0 fusion.14
  602.3 95.5 %while.19 = (s32[]{:T(128)}, f32[64,7]{0,1:T(8,128)S(1)}, f32[64,7]{0,1:T(8,128)S(1)}, f32[64,7,128]{2,1,0:T(8,128)S(1)}, f32[64,64,7]{1,2,0:T(8,128)S(1)}, /*in...) while((s32[]{:T(128)}, f32[64,7]{0,1:T(8,128)S(1)}, ...), condition=%wide.region_12.13_spmd, body=%wide.region_11.12_spmd.sunk | while | flops 174725 | bytes 1172119 | solution.py:20
  603.8 1.0 constant_dynamic-slice_fusion.4
  606.9 1.0 constant_dynamic-slice_fusion.4
  609.9 1.0 constant_dynamic-slice_fusion.4
  698.2 80.7 %all-gather.6 = bf16[64,1,896]{2,1,0:T(2,128)(2,1)S(1)} all-gather(bf16[1,1,896]{2,1,0:T(2,128)(2,1)S(1)} %convert_bitcast_fusion), channel_id=1, replica_groups=mesh['nodes'=64,'heads'=8] {'nodes'}, dimensions={0}, use_global_device_ids=true | all-gather | bytes 116480 | tf_op jit(solution)/shard_map/all_gather | solution.py:182
  779.1 23.6 %all-reduce.1 = bf16[64,112]{1,0:T(8,128)(2,1)S(1)} all-reduce(f32[64,112]{1,0:T(8,128)S(1)} %fusion.10), channel_id=7, replica_groups=mesh['nodes'=64,'heads'=8] {'heads'}, use_global_device_ids=true, to_apply=%region_16.17.clone | all-reduce | flops 7168 | bytes 43008
  (358 shorter events, 103.2 us)
Async XLA Ops:
  6.5 417.5 %copy-start = (bf16[4,128,7,128]{3,1,2,0:T(8,128)(2,1)S(1)}, bf16[4,128,7,128]{3,1,2,0:T(8,128)(2,1)}, u32[]{:S(2)}) copy-start(bf16[4,128,7,128]{3,1,2,0:T(8,128)(2,1)} %param.20) | copy-start | bytes 2752516
  6.5 772.4 %copy-start.1 = (bf16[896,112]{0,1:T(8,128)(2,1)S(1)}, bf16[896,112]{0,1:T(8,128)(2,1)}, u32[]{:S(2)}) copy-start(bf16[896,112]{0,1:T(8,128)(2,1)} %param.19) | copy-start | bytes 602116
  12.4 32.1 %all-to-all-start = ((bf16[1,64,112]{2,0,1:T(2,128)(2,1)}), bf16[1,64,112]{2,0,1:T(2,128)(2,1)S(1)}, u32[]{:S(2)}, u32[]{:S(2)}) async-start(bf16[1,64,112]{2,0,1:T(2,128)(2,1)} %all_to_all.15), calls=%async_computation | async-start | bytes 65536 | tf_op jit(solution)/shard_map/all_to_all | solution.py:121
  31.0 570.1 %all-gather.9.cloned.1.call-start = ((), (), s32[]{:S(2)}) async-start(), calls=%async_computation.1 | async-start | bytes 14909440 | tf_op jit(solution)/shard_map/all_gather | solution.py:15
Sparse Core Ops, SparseCore 0:
  426.9 174.2 all-gather.8
where the time goes:
time: 813 us; the launch traced here: 810 us
  blocking collectives  644 us (79%)
  local copies, waits for them, and re-layouts  84.4 us (10%)
  other arithmetic  32.2 us (4%)
  starting transfers between devices  18.7 us (2%)
  between operations  18 us (2%)
    unnamed x2, blocking collectives  281 us
    all_gather x2, blocking collectives, joined(): gathered = jax.tree.map(lambda a: lax.all_gather(a, axis), part)  161 us
    all_gather x1, blocking collectives, on_device(): query_all = lax.all_gather(query_here, 'nodes', axis=0, tiled=True)  121 us
    all_gather x1, blocking collectives, on_device(): lax.all_gather(attended, 'nodes', axis=0, tiled=True)  80.7 us
    dynamic_slice x66, local copies, waits for them, and re-layouts, take(): lax.dynamic_index_in_dim(a, source, 0, False)  61.8 us
    add x63, other arithmetic, combine(): first_part[2] * factor_one[..., None]  19.3 us
    all_to_all x1, starting transfers between devices, on_device(): lax.all_to_all(normed, 'nodes', split_axis=1, concat_axis=0, tiled=True)  18.6 us
  transfers between devices with their start and end apart: 2, of which 2 were waited for; matrix products, arithmetic and copies ran while one was open for 2% of the time, Pallas kernels for 0%

commit v1 on v0

--- a/solution.py
+++ b/solution.py
@@ -1,3 +1,4 @@
+import functools
 import math
 import jax
 import jax.numpy as jnp
@@ -9,6 +10,18 @@
 MIDS = 32
 epsilon = 1e-05
 negative_fill = -1e30
+
+
+def bind_state(panel, dev_axis):
+    return jnp.concatenate(
+        jax.lax.all_to_all(
+            jnp.stack([panel for _ in range(jax.lax.axis_size(dev_axis))], 0), dev_axis, 0, 0
+        ),
+        0,
+    )
+
+
+group_knots = functools.partial(bind_state, dev_axis="nodes")
 
 
 def joined(part, axis, combine):
@@ -131,7 +144,7 @@
     query_here = mixed_rows[:, :, 0]
     key_new = mixed_rows[:, :, 1]
     value_new = mixed_rows[:, :, 2]
-    query_all = lax.all_gather(query_here, "nodes", axis=0, tiled=True)
+    query_all = group_knots(query_here)
     root_node, mid_node, root_len, finish = tree_rows(piece_node, mid_parent, leaf_parent, leaf_len)
     chosen = node_index * seg_dev + jnp.arange(seg_dev, dtype=jnp.int32)
     node_block, rank_block = piece_rank(piece_node, chosen)

time: 813 us -> 737 us (0.907)
  blocking collectives: 644 us -> 523 us
  starting transfers between devices: 18.7 us -> 47.7 us
  waiting for transfers between devices: 5.58 us -> 19.7 us
    all_gather x1 -> x0, blocking collectives: 121 us -> none  [on_device(): query_all = lax.all_gather(query_here, 'nodes', axis=0, tiled=True)]
    all_to_all x0 -> x1, starting transfers between devices: none -> 29 us  [bind_state(): jax.lax.all_to_all(jnp.stack([panel for _ in range(jax.lax.axis_size(dev_...]
    all_to_all x0 -> x1, waiting for transfers between devices: none -> 13.5 us  [bind_state(): jax.lax.all_to_all(jnp.stack([panel for _ in range(jax.lax.axis_size(dev_...]
  transfers between devices with their start and end apart: 2 -> 3, of which waited for: 2 -> 2; matrix products, arithmetic and copies ran while one was open for 2% -> 2% of each run, Pallas kernels for 0% -> 0%
where the time goes in v1:
time: 737 us; the launch traced here: 734 us
  blocking collectives  523 us (71%)
  local copies, waits for them, and re-layouts  85.1 us (12%)
  starting transfers between devices  47.7 us (6%)
  other arithmetic  32.4 us (4%)
  waiting for transfers between devices  19.7 us (3%)
  between operations  18 us (2%)
    unnamed x2, blocking collectives  282 us
    all_gather x2, blocking collectives, joined(): gathered = jax.tree.map(lambda a: lax.all_gather(a, axis), part)  161 us
    all_gather x1, blocking collectives, on_device(): lax.all_gather(attended, 'nodes', axis=0, tiled=True)  80.6 us
    dynamic_slice x66, local copies, waits for them, and re-layouts, take(): lax.dynamic_index_in_dim(a, source, 0, False)  61.8 us
    all_to_all x1, starting transfers between devices, bind_state(): jax.lax.all_to_all(jnp.stack([panel for _ in range(jax.lax.axis_size(dev_...  29 us
    add x63, other arithmetic, combine(): first_part[2] * factor_one[..., None]  19.5 us
    all_to_all x1, starting transfers between devices, on_device(): lax.all_to_all(normed, 'nodes', split_axis=1, concat_axis=0, tiled=True)  18.6 us
  transfers between devices with their start and end apart: 3, of which 2 were waited for; matrix products, arithmetic and copies ran while one was open for 2% of the time, Pallas kernels for 0%

profile of v1, /device:TPU:2, one launch (start us, length us, event | category | flops | bytes accessed | tf_op | source)
XLA Modules:
  0.0 733.9 jit_solution(4371355274535095348)
XLA Ops:
  6.5 1.5 convert_reduce_fusion.3
  8.7 1.4 multiply_reduce_fusion
  12.4 18.6 %all-to-all-start = ((bf16[1,64,112]{2,0,1:T(2,128)(2,1)}), bf16[1,64,112]{2,0,1:T(2,128)(2,1)S(1)}, u32[]{:S(2)}, u32[]{:S(2)}) async-start(bf16[1,64,112]{2,0,1:T(2,128)(2,1)} %all_to_all.19), calls=%async_computation | async-start | bytes 65536 | tf_op jit(solution)/shard_map/all_to_all | solution.py:134
  35.8 1.1 copy.80
  37.0 1.3 dynamic-slice
  38.3 6.2 all-to-all-done
  44.7 258.1 %all-reduce.3 = bf16[64,2688]{1,0:T(8,128)(2,1)S(1)} all-reduce(f32[64,2688]{1,0:T(8,128)S(1)} %fusion.19), channel_id=5, replica_groups=mesh['nodes'=64,'heads'=8] {'nodes'}, use_global_device_ids=true, to_apply=%region_8.9.clone | all-reduce | flops 172032 | bytes 1032192
  304.2 29.0 %all-to-all-start.1 = ((bf16[64,1,7,128]{3,2,1,0:T(8,128)(2,1)}), bf16[64,1,7,128]{3,2,1,0:T(8,128)(2,1)S(1)}, u32[]{:S(2)}, u32[]{:S(2)}) async-start(bf16[64,1,7,128]{3,2,1,0:T(8,128)(2,1)} %stack.3), calls=%async_computation.1 | async-start | bytes 262144 | tf_op jit(solution)/shard_map/all_to_all | solution.py:17
  334.3 13.5 %all-to-all-done.1 = bf16[64,1,7,128]{3,2,1,0:T(8,128)(2,1)S(1)} async-done(((bf16[64,1,7,128]{3,2,1,0:T(8,128)(2,1)}), bf16[64,1,7,128]{3,2,1,0:T(8,128)(2,1)S(1)}, u32[]{:S(2)}, u32[]{:S(2)}) %all-to-all-start.1) | async-done | bytes 114720 | tf_op jit(solution)/shard_map/all_to_all | solution.py:17
  348.2 2.2 convolution_bitcast_fusion
  350.5 1.2 dynamic_slice.68
  351.7 1.3 dynamic_slice.70
  353.1 1.3 dynamic_slice.69
  357.4 1.3 dynamic-slice.2
  359.4 1.3 compare_and_fusion
  360.7 1.1 fusion.16
  362.2 1.0 fusion.14
  363.3 79.9 %all-gather.3 = f32[64,64,7]{1,2,0:T(8,128)S(1)} all-gather(f32[1,64,7]{1,2,0:T(8,128)S(1)} %bitcast.137), channel_id=2, replica_groups=mesh['nodes'=64,'heads'=8] {'nodes'}, dimensions={0}, use_global_device_ids=true | all-gather | bytes 116480 | tf_op jit(solution)/shard_map/all_gather | solution.py:28
  443.5 81.1 %all-gather.4 = f32[64,64,7]{1,2,0:T(8,128)S(1)} all-gather(f32[1,64,7]{1,2,0:T(8,128)S(1)} %bitcast.139), channel_id=3, replica_groups=mesh['nodes'=64,'heads'=8] {'nodes'}, dimensions={0}, use_global_device_ids=true | all-gather | bytes 116480 | tf_op jit(solution)/shard_map/all_gather | solution.py:28
  525.8 95.7 %while.19 = (s32[]{:T(128)}, f32[64,7]{0,1:T(8,128)S(1)}, f32[64,7]{0,1:T(8,128)S(1)}, f32[64,7,128]{2,1,0:T(8,128)S(1)}, f32[64,64,7]{1,2,0:T(8,128)S(1)}, /*in...) while((s32[]{:T(128)}, f32[64,7]{0,1:T(8,128)S(1)}, ...), condition=%wide.region_12.13_spmd, body=%wide.region_11.12_spmd.sunk | while | flops 174725 | bytes 1172119 | solution.py:33
  527.4 1.0 constant_dynamic-slice_fusion.4
  530.4 1.0 constant_dynamic-slice_fusion.4
  622.0 80.6 %all-gather.5 = bf16[64,1,896]{2,1,0:T(2,128)(2,1)S(1)} all-gather(bf16[1,1,896]{2,1,0:T(2,128)(2,1)S(1)} %convert_bitcast_fusion), channel_id=1, replica_groups=mesh['nodes'=64,'heads'=8] {'nodes'}, dimensions={0}, use_global_device_ids=true | all-gather | bytes 116480 | tf_op jit(solution)/shard_map/all_gather | solution.py:195
  702.8 23.6 %all-reduce.1 = bf16[64,112]{1,0:T(8,128)(2,1)S(1)} all-reduce(f32[64,112]{1,0:T(8,128)S(1)} %fusion.10), channel_id=6, replica_groups=mesh['nodes'=64,'heads'=8] {'heads'}, use_global_device_ids=true, to_apply=%region_16.17.clone | all-reduce | flops 7168 | bytes 43008
  (360 shorter events, 104.7 us)
Async XLA Ops:
  6.5 341.2 %copy-start = (bf16[4,128,7,128]{3,1,2,0:T(8,128)(2,1)S(1)}, bf16[4,128,7,128]{3,1,2,0:T(8,128)(2,1)}, u32[]{:S(2)}) copy-start(bf16[4,128,7,128]{3,1,2,0:T(8,128)(2,1)} %param.20) | copy-start | bytes 2752516
  6.5 696.1 %copy-start.1 = (bf16[896,112]{0,1:T(8,128)(2,1)S(1)}, bf16[896,112]{0,1:T(8,128)(2,1)}, u32[]{:S(2)}) copy-start(bf16[896,112]{0,1:T(8,128)(2,1)} %param.19) | copy-start | bytes 602116
  12.4 32.1 %all-to-all-start = ((bf16[1,64,112]{2,0,1:T(2,128)(2,1)}), bf16[1,64,112]{2,0,1:T(2,128)(2,1)S(1)}, u32[]{:S(2)}, u32[]{:S(2)}) async-start(bf16[1,64,112]{2,0,1:T(2,128)(2,1)} %all_to_all.19), calls=%async_computation | async-start | bytes 65536 | tf_op jit(solution)/shard_map/all_to_all | solution.py:134
  304.2 43.5 %all-to-all-start.1 = ((bf16[64,1,7,128]{3,2,1,0:T(8,128)(2,1)}), bf16[64,1,7,128]{3,2,1,0:T(8,128)(2,1)S(1)}, u32[]{:S(2)}, u32[]{:S(2)}) async-start(bf16[64,1,7,128]{3,2,1,0:T(8,128)(2,1)} %stack.3), calls=%async_computation.1 | async-start | bytes 262144 | tf_op jit(solution)/shard_map/all_to_all | solution.py:17
  333.2 191.4 %all-gather.8.cloned.1.call-start = ((), (), s32[]{:S(2)}) async-start(), calls=%async_computation.2 | async-start | bytes 14909440 | tf_op jit(solution)/shard_map/all_gather | solution.py:28
Sparse Core Ops, SparseCore 0:
  350.6 173.8 all-gather.7
